TPU v7x, 256 devices: a whole 4x4x8 slice. The times are simulated.
256 devices in a mesh: ab: 16 (over z_lo, y, core), cd: 16 (over z_hi, x).
Axes of the slice: x: 4, y: 4, z: 8 (z_hi: 4, z_lo: 2; z = z_hi * 2 + z_lo), core: 2. Of those that a mesh axis runs over, the one named last changes fastest.
Arguments:
- pair_values: bfloat16 [32768, 32768], P('ab', 'cd'), may hold values from -0.046875 to 0.046875
- amplitudes: bfloat16 [64, 800, 800], P('ab', 'cd'), may hold values from -6 to 6
- cd_first: int32 [32768], P('cd'), may hold values from 0 to 799, as said below
- cd_second: int32 [32768], P('cd'), may hold values from 0 to 799, as said below
- live_cols: int32 [16], P('cd'), may hold values from 512 to 2048, as said below
Outputs:
- ladder: bfloat16 [64, 32768], P(None, ('ab', 'cd'))
Inputs may be any that keep to these rules, and one draw needn't show every extreme that they name: `cd_first`: slot n lies in slab s = n // 2048 and its c lies in orbitals s * 50 to (s + 1) * 50 - 1. cd_second[n] >= cd_first[n] for every slot. `live_cols`: slots 0 and 1 of every slab are live.
All inputs are finite; a program needn't handle non-finite values.
Results may differ from a plain program's by a relative error of at most 0.0051.
Values may be sent and summed in bfloat16 or wider, within the bound.
A program may use at most 64 MiB of HBM per device.

v0:
```python
import jax
import jax.numpy as jnp
from jax import lax
from jax.sharding import PartitionSpec as P


def on_device(pair_values, amplitudes, cd_first, cd_second, live_cols):
    slab = lax.axis_index("cd")
    pair_block = amplitudes.shape[0]
    orbit_block = amplitudes.shape[1]
    orbitals = amplitudes.shape[2]
    columns = cd_first.shape[0]
    local_first = cd_first - slab * orbit_block
    own_flat = amplitudes.reshape(pair_block, orbit_block * orbitals)
    direct = jnp.take(own_flat, local_first * orbitals + cd_second, axis=1)
    whole = lax.all_gather(amplitudes, "cd", axis=1, tiled=True)
    whole_flat = whole.reshape(pair_block, orbitals * orbitals)
    crossed = jnp.take(whole_flat, cd_second * orbitals + cd_first, axis=1)
    live_count = live_cols[0]
    slots = jnp.arange(columns, dtype=jnp.int32)
    live = (slots < live_count).astype(jnp.float32)
    half = jnp.where(cd_first == cd_second, jnp.float32(0.5), jnp.float32(1.0))
    weight = half * live
    packed = ((direct.astype(jnp.float32) + crossed.astype(jnp.float32)) * weight[None, :]).astype(
        jnp.bfloat16
    )
    contract = (((1,), (1,)), ((), ()))
    partial_sums = lax.dot_general(
        lax.all_gather(packed, "ab", axis=0, tiled=True),
        pair_values,
        contract,
        preferred_element_type=jnp.float32,
    )
    return lax.psum_scatter(partial_sums, "cd", scatter_dimension=1, tiled=True).astype(
        jnp.bfloat16
    )


def solution(mesh):
    placed = (P("ab", "cd"), P("ab", "cd", None), P("cd"), P("cd"), P("cd"))
    return jax.shard_map(
        on_device, mesh=mesh, in_specs=placed, out_specs=P(None, ("ab", "cd")), check_vma=False
    )
```

profile of v0, /device:TPU:8, one launch (start us, length us, event | category | flops | bytes accessed | tf_op | source)
XLA Modules:
  0.0 270.1 jit_solution(3929936494071455766)
XLA Ops:
  6.5 0.0 copy-start.1
  6.5 0.0 copy-start
  6.5 0.0 all-gather.3.cloned.1.call-start
  6.5 0.7 all-gather.3.cloned.1.call-update
  7.3 0.0 reduce-scatter.2.cloned.1.call-start
  7.3 8.0 %copy.29 = bf16[4,50,800]{0,2,1:T(8,128)(2,1)} copy(bf16[4,50,800]{2,0,1:T(4,128)(2,1)} %param.6) | data formatting | bytes 640000 | tf_op args[1]
  15.9 0.0 copy-done.1
  15.9 0.0 copy-done
  16.0 10.8 %gather_fusion = bf16[2048,4]{1,0:T(8,128)(2,1)S(1)} fusion(bf16[4,40000]{0,1:T(8,128)(2,1)} %bitcast.9, s32[2048]{0:T(1024)S(1)} %get-tuple-element.7), kind=kCustom, calls=%fused_computation | custom fusion | bytes 40960 | tf_op jit(solution)/shard_map/jit(_take)/gather | solution.py:15
  26.8 0.2 copy.30
  27.0 70.5 %all-gather.3.cloned.1.call-done = bf16[4,800,800]{2,0,1:T(4,128)(2,1)} async-done(((bf16[4,50,800]{2,0,1:T(4,128)(2,1)}), bf16[4,800,800]{2,0,1:T(4,128)(2,1)}) %all-gather.3.cloned.1.call-update) | async-done | bytes 5120016 | tf_op jit(solution)/shard_map/all_gather | solution.py:16
  97.6 5.8 %copy.31 = bf16[4,800,800]{2,1,0:T(8,128)(2,1)} copy(bf16[4,800,800]{2,0,1:T(4,128)(2,1)} %all-gather.3.cloned.1.call-done) | data formatting | bytes 10240000 | tf_op jit(solution)/shard_map/all_gather | solution.py:16
  103.4 12.8 %reshape.39 = bf16[2560000]{0:T(1024)(128)(2,1)} reshape(bf16[4,800,800]{2,1,0:T(8,128)(2,1)} %copy.31) | data formatting | bytes 10240000
  116.2 6.6 %reshape.18 = bf16[4,640000]{1,0:T(4,128)(2,1)} reshape(bf16[2560000]{0:T(1024)(128)(2,1)} %reshape.39) | data formatting | bytes 10240000 | tf_op jit(solution)/shard_map/reshape | solution.py:17
  122.8 23.2 %gather_fusion.1 = bf16[2048,4]{0,1:T(4,128)(2,1)S(1)} fusion(bf16[4,640000]{1,0:T(4,128)(2,1)} %reshape.18, s32[2048]{0:T(1024)S(1)} %get-tuple-element.8), kind=kCustom, calls=%fused_computation.1 | custom fusion | bytes 40960 | tf_op jit(solution)/shard_map/jit(_take)/gather | solution.py:18
  146.1 24.5 %all-gather = bf16[16,4,2048]{2,1,0:T(4,128)(2,1)S(1)} all-gather(bf16[1,4,2048]{2,1,0:T(4,128)(2,1)S(1)} %fusion), channel_id=1, replica_groups=mesh['ab'=16,'cd'=16] {'ab'}, dimensions={0}, use_global_device_ids=true | all-gather | bytes 278528 | tf_op jit(solution)/shard_map/all_gather | solution.py:29
  170.6 0.1 reshape.38
  170.7 6.8 %fusion.1 = f32[64,2048]{1,0:T(8,128)} fusion(bf16[64,2048]{1,0:T(8,128)(2,1)S(1)} %reshape.38, bf16[2048,2048]{1,0:T(8,128)(2,1)} %param.5), kind=kOutput, calls=%fused_computation.12 | convolution fusion | flops 536870912 | bytes 9175040 | tf_op jit(solution)/shard_map/dot_general | solution.py:28
  177.5 0.0 reduce-scatter.2.cloned.1.call-update
  177.5 84.4 %reduce-scatter.2.cloned.1.call-done = f32[64,128]{1,0:T(8,128)} async-done(((f32[64,2048]{1,0:T(8,128)}), f32[64,128]{1,0:T(8,128)}) %reduce-scatter.2.cloned.1.call-update) | async-done | bytes 32784 | tf_op jit(solution)/shard_map/reduce_scatter | solution.py:34
  261.9 1.4 convert_element_type.16
  (4 shorter events, 0.1 us)
Async XLA Ops:
  6.5 9.4 %copy-start.1 = (s32[2048]{0:T(1024)S(1)}, s32[2048]{0:T(1024)}, u32[]{:S(2)}) copy-start(s32[2048]{0:T(1024)} %param.8) | copy-start | bytes 24580
  6.5 9.4 %copy-start = (s32[2048]{0:T(1024)S(1)}, s32[2048]{0:T(1024)}, u32[]{:S(2)}) copy-start(s32[2048]{0:T(1024)} %param.7) | copy-start | bytes 24580
  6.5 91.1 %all-gather.3.cloned.1.call-start = ((), (), s32[]{:S(2)}) async-start(), calls=%async_computation.1 | async-start | bytes 6092800 | tf_op jit(solution)/shard_map/all_gather | solution.py:16
  7.3 254.6 %reduce-scatter.2.cloned.1.call-start = ((), (), s32[]{:S(2)}) async-start(), calls=%async_computation.2 | async-start | bytes 557056 | tf_op jit(solution)/shard_map/reduce_scatter | solution.py:34
Sparse Core Ops, SparseCore 0:
  9.8 87.7 all-gather.2
  177.7 84.2 reduce-scatter.1
where the time goes:
time: 271 us; the launch traced here: 270 us
  waiting for transfers between devices  156 us (58%)
  local copies, waits for them, and re-layouts  67.6 us (25%)
  blocking collectives  24.5 us (9%)
  between operations  14.1 us (5%)
  matrix products  6.83 us (3%)
    reduce_scatter x1, waiting for transfers between devices, on_device(): lax.psum_scatter(partial_sums, 'cd', scatter_dimension=1, tiled=True)  84.4 us
    all_gather x1, waiting for transfers between devices, on_device(): whole = lax.all_gather(amplitudes, 'cd', axis=1, tiled=True)  70.5 us
    all_gather x1, blocking collectives, on_device(): lax.all_gather(packed, 'ab', axis=0, tiled=True)  24.5 us
    gather x1, local copies, waits for them, and re-layouts, on_device(): crossed = jnp.take(whole_flat, cd_second * orbitals + cd_first, axis=1)  23.2 us
    unnamed x7, local copies, waits for them, and re-layouts  20.9 us
    gather x2, local copies, waits for them, and re-layouts, on_device(): direct = jnp.take(own_flat, local_first * orbitals + cd_second, axis=1)  11 us
    dot_general x1, matrix products, on_device(): lax.dot_general(lax.all_gather(packed, 'ab', axis=0, tiled=True), pair_va...  6.83 us
    reshape x1, local copies, waits for them, and re-layouts, on_device(): whole_flat = whole.reshape(pair_block, orbitals * orbitals)  6.61 us
  transfers between devices with their start and end apart: 2, of which 2 were waited for; matrix products, arithmetic and copies ran while one was open for 7% of the time, Pallas kernels for 0%

commit v1 on v0

--- a/solution.py
+++ b/solution.py
@@ -2,6 +2,11 @@
 import jax.numpy as jnp
 from jax import lax
 from jax.sharding import PartitionSpec as P
+
+
+def all_by_exchange(x, axis, d):
+    sent = jnp.stack([x] * lax.axis_size(axis))
+    return jnp.concatenate(lax.all_to_all(sent, axis, 0, 0), axis=d)
 
 
 def on_device(pair_values, amplitudes, cd_first, cd_second, live_cols):
@@ -26,10 +31,7 @@
     )
     contract = (((1,), (1,)), ((), ()))
     partial_sums = lax.dot_general(
-        lax.all_gather(packed, "ab", axis=0, tiled=True),
-        pair_values,
-        contract,
-        preferred_element_type=jnp.float32,
+        all_by_exchange(packed, "ab", 0), pair_values, contract, preferred_element_type=jnp.float32
     )
     return lax.psum_scatter(partial_sums, "cd", scatter_dimension=1, tiled=True).astype(
         jnp.bfloat16

time: 271 us -> 264 us (0.974)
  blocking collectives: 24.5 us -> 18 us
    all_gather x1 -> x0, blocking collectives: 24.5 us -> none  [on_device(): lax.all_gather(packed, 'ab', axis=0, tiled=True)]
    all_to_all x0 -> x1, blocking collectives: none -> 18 us  [all_by_exchange(): return jnp.concatenate(lax.all_to_all(sent, axis, 0, 0), axis=d)]
    unnamed x7 -> x6, local copies, waits for them, and re-layouts: 20.9 us -> 20.8 us
where the time goes in v1:
time: 264 us; the launch traced here: 263 us
  waiting for transfers between devices  155 us (59%)
  local copies, waits for them, and re-layouts  67.7 us (26%)
  blocking collectives  18 us (7%)
  between operations  14.1 us (5%)
  matrix products  6.83 us (3%)
    reduce_scatter x1, waiting for transfers between devices, on_device(): lax.psum_scatter(partial_sums, 'cd', scatter_dimension=1, tiled=True)  83.9 us
    all_gather x1, waiting for transfers between devices, on_device(): whole = lax.all_gather(amplitudes, 'cd', axis=1, tiled=True)  70.5 us
    gather x1, local copies, waits for them, and re-layouts, on_device(): crossed = jnp.take(whole_flat, cd_second * orbitals + cd_first, axis=1)  23.2 us
    unnamed x6, local copies, waits for them, and re-layouts  20.8 us
    all_to_all x1, blocking collectives, all_by_exchange(): return jnp.concatenate(lax.all_to_all(sent, axis, 0, 0), axis=d)  18 us
    gather x2, local copies, waits for them, and re-layouts, on_device(): direct = jnp.take(own_flat, local_first * orbitals + cd_second, axis=1)  11 us
    dot_general x1, matrix products, on_device(): lax.dot_general(all_by_exchange(packed, 'ab', 0), pair_values, contract,...  6.83 us
    reshape x1, local copies, waits for them, and re-layouts, on_device(): whole_flat = whole.reshape(pair_block, orbitals * orbitals)  6.61 us
  transfers between devices with their start and end apart: 2, of which 2 were waited for; matrix products, arithmetic and copies ran while one was open for 7% of the time, Pallas kernels for 0%

profile of v1, /device:TPU:8, one launch (start us, length us, event | category | flops | bytes accessed | tf_op | source)
XLA Modules:
  0.0 263.2 jit_solution(13937318981297233874)
XLA Ops:
  6.5 0.0 copy-start.1
  6.5 0.0 copy-start
  6.5 0.0 all-gather.2.cloned.1.call-start
  6.5 0.7 all-gather.2.cloned.1.call-update
  7.3 0.0 reduce-scatter.2.cloned.1.call-start
  7.3 8.0 %copy.22 = bf16[4,50,800]{0,2,1:T(8,128)(2,1)} copy(bf16[4,50,800]{2,0,1:T(4,128)(2,1)} %param.6) | data formatting | bytes 640000 | tf_op args[1]
  15.9 0.0 copy-done.1
  15.9 0.0 copy-done
  16.0 10.8 %gather_fusion = bf16[2048,4]{1,0:T(8,128)(2,1)S(1)} fusion(bf16[4,40000]{0,1:T(8,128)(2,1)} %bitcast.7, s32[2048]{0:T(1024)S(1)} %get-tuple-element.7), kind=kCustom, calls=%fused_computation | custom fusion | bytes 40960 | tf_op jit(solution)/shard_map/jit(_take)/gather | solution.py:20
  26.8 0.2 copy.23
  27.0 70.5 %all-gather.2.cloned.1.call-done = bf16[4,800,800]{2,0,1:T(4,128)(2,1)} async-done(((bf16[4,50,800]{2,0,1:T(4,128)(2,1)}), bf16[4,800,800]{2,0,1:T(4,128)(2,1)}) %all-gather.2.cloned.1.call-update) | async-done | bytes 5120016 | tf_op jit(solution)/shard_map/all_gather | solution.py:21
  97.6 5.8 %copy.24 = bf16[4,800,800]{2,1,0:T(8,128)(2,1)} copy(bf16[4,800,800]{2,0,1:T(4,128)(2,1)} %all-gather.2.cloned.1.call-done) | data formatting | bytes 10240000 | tf_op jit(solution)/shard_map/all_gather | solution.py:21
  103.4 12.8 %reshape.71 = bf16[2560000]{0:T(1024)(128)(2,1)} reshape(bf16[4,800,800]{2,1,0:T(8,128)(2,1)} %copy.24) | data formatting | bytes 10240000
  116.2 6.6 %reshape.51 = bf16[4,640000]{1,0:T(4,128)(2,1)} reshape(bf16[2560000]{0:T(1024)(128)(2,1)} %reshape.71) | data formatting | bytes 10240000 | tf_op jit(solution)/shard_map/reshape | solution.py:22
  122.8 23.2 %gather_fusion.1 = bf16[2048,4]{0,1:T(4,128)(2,1)S(1)} fusion(bf16[4,640000]{1,0:T(4,128)(2,1)} %reshape.51, s32[2048]{0:T(1024)S(1)} %get-tuple-element.8), kind=kCustom, calls=%fused_computation.1 | custom fusion | bytes 40960 | tf_op jit(solution)/shard_map/jit(_take)/gather | solution.py:23
  146.1 0.1 stack.2
  146.2 18.0 %all_to_all.5 = bf16[16,4,2048]{2,1,0:T(4,128)(2,1)S(1)} all-to-all(bf16[16,4,2048]{2,1,0:T(4,128)(2,1)S(1)} %stack.2), channel_id=1, replica_groups=mesh['ab'=16,'cd'=16] {'ab'}, dimensions={0} | all-to-all | bytes 524288 | tf_op jit(solution)/shard_map/all_to_all | solution.py:9
  164.2 0.1 reshape.52
  164.3 6.8 %fusion.1 = f32[64,2048]{1,0:T(8,128)} fusion(bf16[64,2048]{1,0:T(8,128)(2,1)S(1)} %reshape.52, bf16[2048,2048]{1,0:T(8,128)(2,1)} %param.5), kind=kOutput, calls=%fused_computation.12 | convolution fusion | flops 536870912 | bytes 9175040 | tf_op jit(solution)/shard_map/dot_general | solution.py:33
  171.1 0.0 reduce-scatter.2.cloned.1.call-update
  171.1 83.9 %reduce-scatter.2.cloned.1.call-done = f32[64,128]{1,0:T(8,128)} async-done(((f32[64,2048]{1,0:T(8,128)}), f32[64,128]{1,0:T(8,128)}) %reduce-scatter.2.cloned.1.call-update) | async-done | bytes 32784 | tf_op jit(solution)/shard_map/reduce_scatter | solution.py:36
  255.0 1.4 convert_element_type.22
  (4 shorter events, 0.1 us)
Async XLA Ops:
  6.5 9.4 %copy-start.1 = (s32[2048]{0:T(1024)S(1)}, s32[2048]{0:T(1024)}, u32[]{:S(2)}) copy-start(s32[2048]{0:T(1024)} %param.8) | copy-start | bytes 24580
  6.5 9.4 %copy-start = (s32[2048]{0:T(1024)S(1)}, s32[2048]{0:T(1024)}, u32[]{:S(2)}) copy-start(s32[2048]{0:T(1024)} %param.7) | copy-start | bytes 24580
  6.5 91.1 %all-gather.2.cloned.1.call-start = ((), (), s32[]{:S(2)}) async-start(), calls=%async_computation.2 | async-start | bytes 6092800 | tf_op jit(solution)/shard_map/all_gather | solution.py:21
  7.3 247.7 %reduce-scatter.2.cloned.1.call-start = ((), (), s32[]{:S(2)}) async-start(), calls=%async_computation.3 | async-start | bytes 557056 | tf_op jit(solution)/shard_map/reduce_scatter | solution.py:36
Sparse Core Ops, SparseCore 0:
  9.8 87.7 all-gather.1
  171.2 83.6 reduce-scatter.1
